TPU v7x, 512 devices: a whole 4x8x8 slice. The times are simulated.
512 devices in a mesh: cand: 64 (over x, z, core), feat: 8 (over y).
Axes of the slice: x: 4, y: 8, z: 8, core: 2. Of those that a mesh axis runs over, the one named last changes fastest.
Arguments:
- behaviour: float32 [65536, 4096], P('cand', 'feat'), may hold values from 0.2 to 4500, as said below
- panel: float32 [4096, 64], P('feat'), may hold values from -6 to 6
Outputs:
- left_vectors: float32 [65536, 64], P('cand')
- right_vectors: float32 [4096, 64], P('feat')
Inputs may be any that keep to these rules, and one draw needn't show every extreme that they name: `behaviour`: every entry is positive.
All inputs are finite; a program needn't handle non-finite values.
Results may differ from a plain program's by a relative error of at most 0.00017.
Values sent between devices are 32-bit elements; how exact they have to be, the bound alone decides.
No kernel may reach another device: no remote copies, remote signals or barrier semaphores. Data moves between devices by JAX's collectives and lax.ppermute only.
A program may use at most 64 MiB of HBM per device.

v0:
```python
import jax
import jax.numpy as jnp
from jax import lax
from jax.sharding import PartitionSpec as P


def orthonormal(raw_panel, gram):
    factor = jnp.linalg.cholesky(gram)
    return lax.linalg.triangular_solve(
        factor, raw_panel, left_side=False, lower=True, transpose_a=True
    )


def body(behaviour, panel):
    highest = lax.Precision.HIGHEST
    row_part = jnp.sum(behaviour, axis=1)
    col_part = jnp.sum(behaviour, axis=0)
    col_deg = lax.psum(col_part, "cand")
    col_scale = lax.rsqrt(col_deg)
    partial_value = jnp.dot(
        behaviour, panel * col_scale[:, None], precision=highest, preferred_element_type=jnp.float32
    )
    row_deg = lax.psum(row_part, "feat")
    partial_value = partial_value * lax.rsqrt(row_deg)[:, None]
    raw_panel = lax.psum(partial_value, "feat")
    row_scale = lax.rsqrt(row_deg)
    gram_local = jnp.dot(
        raw_panel.T, raw_panel, precision=highest, preferred_element_type=jnp.float32
    )
    gram = lax.psum(gram_local, "cand")
    left_vectors = orthonormal(raw_panel, gram)
    weighted = left_vectors * row_scale[:, None]
    right_part = lax.dot_general(
        behaviour,
        weighted,
        (((0,), (0,)), ((), ())),
        precision=highest,
        preferred_element_type=jnp.float32,
    )
    right_vectors = lax.psum(right_part, "cand") * col_scale[:, None]
    return (left_vectors, right_vectors)


def solution(mesh):
    in_specs = (P("cand", "feat"), P("feat", None))
    out_specs = (P("cand", None), P("feat", None))
    return jax.shard_map(body, mesh=mesh, in_specs=in_specs, out_specs=out_specs, check_vma=False)
```

profile of v0, /device:TPU:1, one launch (start us, length us, event | category | flops | bytes accessed | tf_op | source)
XLA Modules:
  0.0 687.1 jit_solution(3802873574680506946)
XLA Ops:
  7.2 0.0 copy-start
  7.2 0.0 all-reduce.3.cloned.1.call-start
  7.2 2.0 fusion.9
  9.2 131.2 %psum.35 = f32[512]{0:T(512)S(1)} all-reduce(f32[512]{0:T(512)S(1)} %get-tuple-element.2), channel_id=1, replica_groups=mesh['cand'=64,'feat'=8] {'cand'}, use_global_device_ids=true, to_apply=%region_1.0 | all-reduce | flops 512 | bytes 4096 | tf_op jit(solution)/shard_map/psum | solution.py:18
  140.4 13.9 %psum.36 = f32[1024]{0:T(1024)S(1)} all-reduce(f32[1024]{0:T(1024)S(1)} %get-tuple-element.3), channel_id=1, replica_groups=mesh['cand'=64,'feat'=8] {'feat'}, use_global_device_ids=true, to_apply=%region_3.0 | all-reduce | flops 1024 | bytes 8192 | tf_op jit(solution)/shard_map/psum | solution.py:23
  154.2 0.0 copy-done
  154.2 3.7 fusion
  158.0 0.0 all-reduce.3.cloned.1.call-update
  158.0 0.0 all-reduce.5.cloned.1.call-start
  158.0 72.0 %all-reduce.3.cloned.1.call-done = f32[1024,64]{0,1:T(8,128)} async-done(((f32[1024,64]{0,1:T(8,128)}), f32[1024,64]{0,1:T(8,128)}) %all-reduce.3.cloned.1.call-update) | async-done | bytes 262160 | tf_op jit(solution)/shard_map/psum | solution.py:25
  230.1 1.4 fusion.10
  231.4 247.6 %psum.38 = f32[64,64]{0,1:T(8,128)S(1)} all-reduce(f32[64,64]{0,1:T(8,128)S(1)} %fusion.10), channel_id=1, replica_groups=mesh['cand'=64,'feat'=8] {'cand'}, use_global_device_ids=true, to_apply=%region_5.0 | all-reduce | flops 4096 | bytes 32768 | tf_op jit(solution)/shard_map/psum | solution.py:30
  479.0 0.1 copy.5
  479.1 5.8 cholesky.16
  485.0 0.6 compare_reduce_fusion
  485.6 0.7 fusion.5
  486.3 4.9 custom-call.6
  491.2 1.4 fusion.6
  492.6 0.0 copy-start.1
  492.6 2.0 convolution_bitcast_fusion
  494.6 0.0 all-reduce.5.cloned.1.call-update
  494.6 184.1 %all-reduce.5.cloned.1.call-done = f32[512,64]{0,1:T(8,128)} async-done(((f32[512,64]{0,1:T(8,128)}), f32[512,64]{0,1:T(8,128)}) %all-reduce.5.cloned.1.call-update) | async-done | bytes 131088 | tf_op jit(solution)/shard_map/psum | solution.py:40
  678.7 1.6 broadcast_multiply_fusion
  680.3 0.0 copy-done.1
  (4 shorter events, 0.1 us)
Async XLA Ops:
  7.2 147.1 %copy-start = (f32[1024,512]{1,0:T(8,128)S(1)}, f32[1024,512]{1,0:T(8,128)}, u32[]{:S(2)}) copy-start(f32[1024,512]{1,0:T(8,128)} %param.2) | copy-start | bytes 6291460
  7.2 222.9 %all-reduce.3.cloned.1.call-start = ((), (), s32[]{:S(2)}) async-start(), calls=%async_computation | async-start | bytes 524288 | tf_op jit(solution)/shard_map/psum | solution.py:25
  158.0 520.7 %all-reduce.5.cloned.1.call-start = ((), (), s32[]{:S(2)}) async-start(), calls=%async_computation.1 | async-start | bytes 262144 | tf_op jit(solution)/shard_map/psum | solution.py:40
  492.6 187.7 %copy-start.1 = (f32[1024,64]{0,1:T(8,128)}, f32[1024,64]{0,1:T(8,128)S(1)}, u32[]{:S(2)}) copy-start(f32[1024,64]{0,1:T(8,128)S(1)} %fusion.6) | copy-start | bytes 786436
Sparse Core Ops, SparseCore 0:
  158.1 71.8 all-reduce.2
  494.8 183.9 all-reduce.4
where the time goes:
time: 687 us
  blocking collectives  393 us (57%)
  waiting for transfers between devices  256 us (37%)
  other arithmetic  15.6 us (2%)
  between operations  14.1 us (2%)
  matrix products  8.55 us (1%)
    psum x1, blocking collectives, body(): gram = lax.psum(gram_local, 'cand')  248 us
    psum x1, waiting for transfers between devices, body(): right_vectors = lax.psum(right_part, 'cand') * col_scale[:, None]  184 us
    psum x1, blocking collectives, body(): col_deg = lax.psum(col_part, 'cand')  131 us
    psum x1, waiting for transfers between devices, body(): raw_panel = lax.psum(partial_value, 'feat')  72 us
    psum x1, blocking collectives, body(): row_deg = lax.psum(row_part, 'feat')  13.9 us
  transfers between devices with their start and end apart: 2, of which 2 were waited for; matrix products, arithmetic and copies ran while one was open for 0% of the time, Pallas kernels for 0%

commit v1 on v0

v1 whole, which is shorter than its diff:
```python
import jax
import jax.numpy as jnp
from jax import lax
from jax.sharding import PartitionSpec as P

RANK = 64


def dot(a, b, dims):
    return lax.dot_general(
        a, b, (dims, ((), ())), precision=lax.Precision.HIGHEST, preferred_element_type=jnp.float32
    )


def exchange(x, axis):
    return lax.all_to_all(x, axis, 0, 0)


def spread(x, axis, n):
    return exchange(jnp.broadcast_to(x[None], (n,) + x.shape), axis)


def body(behaviour, panel):
    cands, feats = lax.axis_size("cand"), lax.axis_size("feat")
    rows, cols = behaviour.shape
    row_part = jnp.sum(behaviour, axis=1)
    col_part = jnp.sum(behaviour, axis=0)
    col_deg = jnp.sum(spread(col_part.reshape(-1, 128), "cand", cands), axis=0).reshape(cols)
    col_scale = lax.rsqrt(col_deg)

    part = dot(panel.T * col_scale[None, :], behaviour, ((1,), (1,)))
    part = jnp.concatenate([part, row_part[None, :], jnp.zeros((7, rows), jnp.float32)], axis=0)
    part = part.reshape(RANK + 8, feats, rows // feats).transpose(1, 0, 2)
    mine = jnp.sum(exchange(part, "feat"), axis=0)
    scale = lax.rsqrt(mine[RANK : RANK + 1])
    mine = jnp.concatenate([mine[:RANK] * scale, jnp.broadcast_to(scale, (8,) + scale.shape[1:])], axis=0)
    whole = spread(mine, "feat", feats).transpose(1, 0, 2).reshape(RANK + 8, rows)
    raw, row_scale = whole[:RANK], whole[RANK : RANK + 1]

    gram = dot(raw, raw, ((1,), (1,)))
    right = dot(raw * row_scale, behaviour, ((1,), (0,)))
    gram = jnp.pad(gram, ((0, 0), (0, 128 - RANK)))
    both = jnp.concatenate([right.reshape(RANK, -1, 128), gram[:, None, :]], axis=1)
    line = jnp.sum(exchange(both, "cand"), axis=0)
    both = spread(line, "cand", cands)
    gram = both[:, -1, :RANK]
    right = both[:, :-1, :].reshape(RANK, cols) * col_scale[None, :]
    factor = jnp.linalg.cholesky(gram)
    inverse = lax.linalg.triangular_solve(
        factor, jnp.eye(RANK, dtype=jnp.float32), left_side=True, lower=True
    )
    left = dot(inverse, raw, ((1,), (0,)))
    right = dot(inverse, right, ((1,), (0,)))
    return (left.T, right.T)


def solution(mesh):
    in_specs = (P("cand", "feat"), P("feat", None))
    out_specs = (P("cand", None), P("feat", None))
    return jax.shard_map(body, mesh=mesh, in_specs=in_specs, out_specs=out_specs, check_vma=False)
```

time: 687 us -> 119 us (0.17)
  blocking collectives: 393 us -> 55.5 us
  waiting for transfers between devices: 256 us -> 19.1 us
  starting transfers between devices: 0.08 us -> 18.2 us
  between operations: 14.1 us -> 0.84 us
    psum x3 -> x0, blocking collectives: 393 us -> none  [the longest x1 248 us: body(): gram = lax.psum(gram_local, 'cand')]
    psum x2 -> x0, waiting for transfers between devices: 256 us -> none  [the longest x1 184 us: body(): right_vectors = lax.psum(right_part, 'cand') * col_scale[:, None]]
    all_to_all x0 -> x3, blocking collectives: none -> 55.5 us  [exchange(): return lax.all_to_all(x, axis, 0, 0)]
    all_to_all x0 -> x2, waiting for transfers between devices: none -> 19.1 us  [exchange(): return lax.all_to_all(x, axis, 0, 0)]
    all_to_all x0 -> x2, starting transfers between devices: none -> 18.2 us  [exchange(): return lax.all_to_all(x, axis, 0, 0)]
  transfers between devices with their start and end apart: 2 -> 2, of which waited for: 2 -> 2; matrix products, arithmetic and copies ran while one was open for 0% -> 2% of each run, Pallas kernels for 0% -> 0%
where the time goes in v1:
time: 119 us
  blocking collectives  55.5 us (47%)
  waiting for transfers between devices  19.1 us (16%)
  starting transfers between devices  18.2 us (15%)
  other arithmetic  14.4 us (12%)
  matrix products  6.85 us (6%)
  local copies, waits for them, and re-layouts  3.91 us (3%)
    all_to_all x3, blocking collectives, exchange(): return lax.all_to_all(x, axis, 0, 0)  55.5 us
    all_to_all x2, waiting for transfers between devices, exchange(): return lax.all_to_all(x, axis, 0, 0)  19.1 us
    all_to_all x2, starting transfers between devices, exchange(): return lax.all_to_all(x, axis, 0, 0)  18.2 us
    dot_general x5, matrix products, dot(): lax.dot_general(a, b, (dims, ((), ())), precision=lax.Precision.HIGHEST,...  6.62 us
    another operation x3, other arithmetic, body(): factor = jnp.linalg.cholesky(gram)  6.52 us
    another operation x2, other arithmetic, body(): lax.linalg.triangular_solve(factor, jnp.eye(RANK, dtype=jnp.float32), lef...  5.55 us
  transfers between devices with their start and end apart: 2, of which 2 were waited for; matrix products, arithmetic and copies ran while one was open for 2% of the time, Pallas kernels for 0%

profile of v1, /device:TPU:1, one launch (start us, length us, event | category | flops | bytes accessed | tf_op | source)
XLA Modules:
  0.0 118.8 jit_solution(13270635713101093686)
XLA Ops:
  0.6 0.0 copy-start
  0.6 0.0 copy-start.2
  0.6 2.0 %fusion.14 = (f32[512]{0:T(512)S(1)}, f32[1024]{0:T(1024)S(1)}) fusion(f32[1024,512]{1,0:T(8,128)} %param.2), kind=kLoop, calls=%fused_computation.33 | loop fusion | flops 1047040 | bytes 2103296 | tf_op jit(solution)/shard_map/reduce_sum | solution.py:27
  2.6 0.7 broadcast_in_dim.16
  3.3 14.8 %all-to-all-start = ((f32[64,4,128]{2,1,0:T(4,128)}), f32[64,4,128]{2,1,0:T(4,128)S(1)}, u32[]{:S(2)}, u32[]{:S(2)}) async-start(f32[64,4,128]{2,1,0:T(4,128)} %broadcast_in_dim.16), calls=%async_computation | async-start | bytes 262144 | tf_op jit(solution)/shard_map/all_to_all | solution.py:16
  18.1 0.1 pad.11.clone
  18.2 10.2 %all-to-all-done = f32[64,4,128]{2,1,0:T(4,128)S(1)} async-done(((f32[64,4,128]{2,1,0:T(4,128)}), f32[64,4,128]{2,1,0:T(4,128)S(1)}, u32[]{:S(2)}, u32[]{:S(2)}) %all-to-all-start) | async-done | bytes 131104 | tf_op jit(solution)/shard_map/all_to_all | solution.py:16
  28.5 0.1 reduce_sum.46
  28.5 0.0 copy-done
  28.5 0.0 copy-done.2
  28.6 2.1 %convolution_bitcast_fusion = f32[8,8,8,128]{3,2,1,0:T(8,128)S(1)} fusion(f32[1024,512]{1,0:T(8,128)S(1)} %copy-done, f32[512,64]{0,1:T(8,128)S(1)} %copy-done.2, f32[512]{0:T(512)S(1)} %rsqrt_bitcast_fusion), kind=kOutput, calls=%fused_computation | convolution fusion | flops 402685952 | bytes 2492416 | tf_op jit(solution)/shard_map/dot_general | solution.py:10
  30.7 0.1 maximum_bitcast_fusion
  30.8 18.8 %all_to_all.25 = f32[8,72,128]{2,1,0:T(8,128)S(1)} all-to-all(f32[8,72,128]{2,1,0:T(8,128)S(1)} %maximum_bitcast_fusion), channel_id=1, replica_groups=mesh['cand'=64,'feat'=8] {'feat'}, dimensions={0} | all-to-all | bytes 589824 | tf_op jit(solution)/shard_map/all_to_all | solution.py:16
  49.7 0.8 broadcast_in_dim.19
  50.4 3.4 %all-to-all-start.2 = ((f32[8,72,128]{2,1,0:T(8,128)}), f32[8,72,128]{2,1,0:T(8,128)S(1)}, u32[]{:S(2)}, u32[]{:S(2)}) async-start(f32[8,72,128]{2,1,0:T(8,128)} %broadcast_in_dim.19), calls=%async_computation.2 | async-start | bytes 589824 | tf_op jit(solution)/shard_map/all_to_all | solution.py:16
  53.9 1.9 %copy.32 = f32[512,1024]{1,0:T(8,128)} copy(f32[512,1024]{0,1:T(8,128)S(1)} %bitcast.49) | data formatting | bytes 4194304 | tf_op jit(solution)/shard_map/dot_general | solution.py:10
  55.7 0.0 copy-start.1
  55.7 8.8 %all-to-all-done.2 = f32[8,72,128]{2,1,0:T(8,128)S(1)} async-done(((f32[8,72,128]{2,1,0:T(8,128)}), f32[8,72,128]{2,1,0:T(8,128)S(1)}, u32[]{:S(2)}, u32[]{:S(2)}) %all-to-all-start.2) | async-done | bytes 294944 | tf_op jit(solution)/shard_map/all_to_all | solution.py:16
  64.6 0.4 convolution_bitcast_fusion.1
  65.0 0.2 copy.27
  65.2 0.0 copy-done.1
  65.2 2.1 %fusion.15 = f32[64,4,128]{2,0,1:T(8,128)S(1)} fusion(f32[64,1024,1]{1,0,2:T(8,128)S(1)} %reshape.44, f32[4,128,1024]{2,1,0:T(8,128)S(1)} %bitcast.50), kind=kOutput, calls=%fused_computation.34 | convolution fusion | flops 402653184 | bytes 2490368 | tf_op jit(solution)/shard_map/dot_general | solution.py:10
  67.4 0.1 copy.29
  67.5 18.9 %all_to_all.26 = f32[64,5,128]{2,1,0:T(8,128)S(1)} all-to-all(f32[64,5,128]{2,1,0:T(8,128)S(1)} %copy.29), channel_id=1, replica_groups=mesh['cand'=64,'feat'=8] {'cand'}, dimensions={0} | all-to-all | bytes 327680 | tf_op jit(solution)/shard_map/all_to_all | solution.py:16
  86.4 0.1 reduce_sum.49
  86.5 17.8 %all_to_all.27 = f32[64,5,128]{2,1,0:T(8,128)S(1)} all-to-all(f32[64,5,128]{2,1,0:T(8,128)S(1)} %broadcast_in_dim.41), channel_id=1, replica_groups=mesh['cand'=64,'feat'=8] {'cand'}, dimensions={0} | all-to-all | bytes 327680 | tf_op jit(solution)/shard_map/all_to_all | solution.py:16
  104.3 0.1 copy.34
  104.4 5.8 %cholesky.17 = f32[64,64]{1,0:T(8,128)S(1)} custom-call(f32[64,64]{1,0:T(8,128)S(1)} %fusion.10), custom_call_target="Cholesky" | custom-call | tf_op jit(solution)/shard_map/jit(cholesky)/cholesky | solution.py:48
  110.3 0.6 compare_reduce_fusion
  110.9 0.7 fusion.9
  111.6 4.9 %custom-call.6 = f32[1,64,64]{1,2,0:T(8,128)S(1)} custom-call(f32[1,64,64]{2,1,0:T(8,128)S(1)} %fusion.9), custom_call_target="InvertDiagBlocksLowerTriangular" | custom-call | tf_op jit(solution)/shard_map/triangular_solve | solution.py:49
  116.5 0.2 fusion.11
  116.8 0.9 fusion.4
  117.7 1.1 fusion
  (18 shorter events, 0.3 us)
Async XLA Ops:
  0.6 27.9 %copy-start = (f32[1024,512]{1,0:T(8,128)S(1)}, f32[1024,512]{1,0:T(8,128)}, u32[]{:S(2)}) copy-start(f32[1024,512]{1,0:T(8,128)} %param.2) | copy-start | bytes 6291460
  0.6 27.9 %copy-start.2 = (f32[512,64]{0,1:T(8,128)S(1)}, f32[512,64]{0,1:T(8,128)}, u32[]{:S(2)}) copy-start(f32[512,64]{0,1:T(8,128)} %param.3) | copy-start | bytes 393220
  3.3 25.2 %all-to-all-start = ((f32[64,4,128]{2,1,0:T(4,128)}), f32[64,4,128]{2,1,0:T(4,128)S(1)}, u32[]{:S(2)}, u32[]{:S(2)}) async-start(f32[64,4,128]{2,1,0:T(4,128)} %broadcast_in_dim.16), calls=%async_computation | async-start | bytes 262144 | tf_op jit(solution)/shard_map/all_to_all | solution.py:16
  50.4 14.1 %all-to-all-start.2 = ((f32[8,72,128]{2,1,0:T(8,128)}), f32[8,72,128]{2,1,0:T(8,128)S(1)}, u32[]{:S(2)}, u32[]{:S(2)}) async-start(f32[8,72,128]{2,1,0:T(8,128)} %broadcast_in_dim.19), calls=%async_computation.2 | async-start | bytes 589824 | tf_op jit(solution)/shard_map/all_to_all | solution.py:16
  55.7 9.5 %copy-start.1 = (f32[512,1024]{1,0:T(8,128)S(1)}, f32[512,1024]{1,0:T(8,128)}, u32[]{:S(2)}) copy-start(f32[512,1024]{1,0:T(8,128)} %copy.32) | copy-start | bytes 6291460

commit v2 on v1

v2 whole, which is shorter than its diff:
```python
import jax
import jax.numpy as jnp
from jax import lax
from jax.experimental import pallas as pl
from jax.experimental.pallas import tpu as pltpu
from jax.sharding import Mesh, PartitionSpec as P

RANK = 64
PAD = RANK + 8
LANES = 128
GRID = (4, 8, 2)
NT = (((1,), (1,)), ((), ()))
NN = (((1,), (0,)), ((), ()))


def split(a):
    high = a.astype(jnp.bfloat16)
    low = (a - high.astype(jnp.float32)).astype(jnp.bfloat16)
    return high, low


def product(a, b, dims):
    m = a[0].shape[0]
    stacked = jnp.concatenate([a[0], a[1]], axis=0)
    full = lax.dot_general(stacked, b[0], dims, preferred_element_type=jnp.float32)
    rest = lax.dot_general(a[0], b[1], dims, preferred_element_type=jnp.float32)
    return full[:m] + (full[m:] + rest)


def call(kernel, out_shape, operands, name, flops, nbytes):
    return pl.pallas_call(
        kernel,
        out_shape=out_shape,
        name=name,
        in_specs=[pl.BlockSpec(memory_space=pltpu.VMEM)] * len(operands),
        out_specs=jax.tree.map(lambda _: pl.BlockSpec(memory_space=pltpu.VMEM), out_shape),
        cost_estimate=pl.CostEstimate(flops=flops, bytes_accessed=nbytes, transcendentals=0),
        compiler_params=pltpu.CompilerParams(vmem_limit_bytes=24 << 20),
    )(*operands)


def column_kernel(b_ref, out_ref):
    copies, parts, _ = out_ref.shape
    sums = jnp.sum(b_ref[...], axis=0, keepdims=True)
    rows = jnp.concatenate([sums[:, LANES * i : LANES * (i + 1)] for i in range(parts)], axis=0)
    out_ref[...] = jnp.broadcast_to(rows[None], out_ref.shape)


def project_kernel(b_ref, panel_ref, sums_ref, out_ref, scale_ref):
    parts = sums_ref.shape[1]
    deg = jnp.sum(sums_ref[...], axis=0)
    deg = jnp.concatenate([deg[i : i + 1] for i in range(parts)], axis=1)
    scale = lax.rsqrt(deg)
    scale_ref[...] = scale
    ones = jnp.ones((PAD - RANK, deg.shape[1]), jnp.float32)
    left = split(jnp.concatenate([panel_ref[...] * scale, ones], axis=0))
    for i in range(out_ref.shape[0]):
        out_ref[i] = product(left, split(b_ref[LANES * i : LANES * (i + 1), :]), NT)


def normalise_kernel(parts_ref, out_ref):
    total = jnp.sum(parts_ref[...], axis=0)
    scale = lax.rsqrt(total[RANK:])
    out = jnp.concatenate([total[:RANK] * scale[:1], scale], axis=0)
    out_ref[...] = jnp.broadcast_to(out[None], out_ref.shape)


def reduce_kernel(b_ref, whole_ref, out_ref):
    chunks = whole_ref.shape[0]
    raw = jnp.concatenate([whole_ref[i, :RANK, :] for i in range(chunks)], axis=1)
    scale = jnp.concatenate([whole_ref[i, RANK : RANK + 1, :] for i in range(chunks)], axis=1)
    cols = b_ref.shape[1]
    out_ref[:, :cols] = product(split(raw * scale), split(b_ref[...]), NN)
    gram = lax.dot_general(
        raw, raw, NT, precision=lax.Precision.HIGHEST, preferred_element_type=jnp.float32
    )
    out_ref[:, cols:] = jnp.concatenate([gram, jnp.zeros((RANK, LANES - RANK), jnp.float32)], axis=1)


def finish_kernel(both_ref, whole_ref, scale_ref, left_ref, right_ref):
    chunks = whole_ref.shape[0]
    cols = scale_ref.shape[1]
    sub = lax.broadcasted_iota(jnp.int32, (8, LANES), 0)
    lane = lax.broadcasted_iota(jnp.int32, (8, LANES), 1)
    work = [
        jnp.where(
            lane < RANK, both_ref[8 * b : 8 * b + 8, cols:], (lane == RANK + 8 * b + sub).astype(jnp.float32)
        )
        for b in range(RANK // 8)
    ]
    roots = [None] * (RANK // 8)
    for k in range(RANK):
        at, s = divmod(k, 8)
        row = work[at][s : s + 1, :]
        pivot = row[:, k : k + 1]
        scaled = row * (1.0 / pivot)
        root = jnp.broadcast_to(lax.rsqrt(pivot), (8, LANES))
        roots[at] = root if s == 0 else jnp.where(sub == s, root, roots[at])
        for b in range(at, RANK // 8):
            column = work[b][:, k : k + 1]
            if b == at:
                column = jnp.where(sub[:, :1] > s, column, 0.0)
            work[b] = work[b] - column * scaled
    inverse = jnp.concatenate([work[b] * roots[b] for b in range(RANK // 8)], axis=0)[:, RANK:]
    inverse = split(inverse)
    for i in range(chunks):
        left_ref[:, LANES * i : LANES * (i + 1)] = product(inverse, split(whole_ref[i, :RANK, :]), NN)
    right_ref[...] = product(inverse, split(both_ref[:, :cols] * scale_ref[...]), NN)


def exchange(x, axis):
    return lax.all_to_all(x, axis, 0, 0)


def spread(x, axis, n):
    return exchange(jnp.broadcast_to(x[None], (n,) + x.shape), axis)


def body(behaviour, panel):
    x, z, core = GRID
    feats = lax.axis_size("feat")
    rows, cols = behaviour.shape
    cands = ("x", "z", "core")
    near = ("x", "core")
    f32 = jnp.float32
    shape = jax.ShapeDtypeStruct

    sums = call(
        column_kernel, shape((x * z * core, cols // LANES, LANES), f32), (behaviour,), "columns", rows * cols, 4 * rows * cols
    )
    sums = exchange(sums, cands)
    part, col_scale = call(
        project_kernel,
        (shape((feats, PAD, rows // feats), f32), shape((1, cols), f32)),
        (behaviour, panel.T, sums),
        "project",
        6 * rows * cols * PAD,
        4 * rows * cols,
    )
    part = exchange(part, "feat")
    mine = call(
        normalise_kernel, shape(part.shape, f32), (part,), "normalise", part.size, 8 * part.size
    )
    whole = exchange(mine, "feat")
    both = call(
        reduce_kernel, shape((RANK, cols + LANES), f32), (behaviour, whole), "reduce", 6 * rows * cols * RANK, 4 * rows * cols
    )
    both = exchange(both.reshape(x * core, -1, cols + LANES), near)
    line = jnp.sum(both, axis=0)
    line = jnp.sum(spread(line, "z", z), axis=0)
    both = spread(line, near, x * core).reshape(RANK, cols + LANES)
    left, right = call(
        finish_kernel,
        (shape((RANK, rows), f32), shape((RANK, cols), f32)),
        (both, whole, col_scale),
        "finish",
        6 * RANK * RANK * (rows + cols),
        8 * RANK * (rows + cols),
    )
    return (left.T, right.T)


def solution(mesh):
    assert GRID[0] * GRID[1] * GRID[2] == mesh.shape["cand"]
    fine = Mesh(mesh.devices.reshape(GRID + (mesh.shape["feat"],)), ("x", "z", "core", "feat"))
    cands = ("x", "z", "core")
    in_specs = (P(cands, "feat"), P("feat", None))
    out_specs = (P(cands, None), P("feat", None))
    return jax.shard_map(body, mesh=fine, in_specs=in_specs, out_specs=out_specs, check_vma=False)
```

time: 119 us -> 100 us (0.84)
  blocking collectives: 55.5 us -> 89.2 us
  waiting for transfers between devices: 19.1 us -> 0 us
  starting transfers between devices: 18.2 us -> 0 us
  other arithmetic: 14.4 us -> 0.03 us
  Pallas kernels: 0 us -> 8.1 us
  matrix products: 6.85 us -> 0 us
  local copies, waits for them, and re-layouts: 3.91 us -> 1.62 us
    all_to_all x3 -> x6, blocking collectives: 55.5 us -> 89.2 us  [exchange(): return lax.all_to_all(x, axis, 0, 0)]
    all_to_all x2 -> x0, waiting for transfers between devices: 19.1 us -> none  [exchange(): return lax.all_to_all(x, axis, 0, 0)]
    all_to_all x2 -> x0, starting transfers between devices: 18.2 us -> none  [exchange(): return lax.all_to_all(x, axis, 0, 0)]
    another operation x5 -> x0, other arithmetic: 12.1 us -> none  [the longest x3 6.52 us: body(): factor = jnp.linalg.cholesky(gram)]
    pallas_call x0 -> x5, Pallas kernels: none -> 8.1 us  [call(): pl.pallas_call(kernel, out_shape=out_shape, name=name, in_specs=[pl.Block...]
    dot_general x5 -> x0, matrix products: 6.62 us -> none  [dot(): lax.dot_general(a, b, (dims, ((), ())), precision=lax.Precision.HIGHEST,...]
    reduce_sum x4 -> x2, other arithmetic: 2.13 us -> 0.03 us  [the longest x1 0.01 us: body(): line = jnp.sum(spread(line, 'z', z), axis=0)]
    dot_general x1 -> x0, local copies, waits for them, and re-layouts: 1.88 us -> none  [dot(): lax.dot_general(a, b, (dims, ((), ())), precision=lax.Precision.HIGHEST,...]
  transfers between devices with their start and end apart: 2 -> 0, of which waited for: 2 -> 0; matrix products, arithmetic and copies ran while one was open for 2% -> 0% of each run, Pallas kernels for 0% -> 0%
where the time goes in v2:
time: 100 us; the launch traced here: 99.6 us
  blocking collectives  89.2 us (89%)
  Pallas kernels  8.1 us (8%)
  local copies, waits for them, and re-layouts  1.62 us (2%)
    all_to_all x6, blocking collectives, exchange(): return lax.all_to_all(x, axis, 0, 0)  89.2 us
    pallas_call x5, Pallas kernels, call(): pl.pallas_call(kernel, out_shape=out_shape, name=name, in_specs=[pl.Block...  8.1 us

profile of v2, /device:TPU:1, one launch (start us, length us, event | category | flops | bytes accessed | tf_op | source)
XLA Modules:
  0.0 99.6 jit_solution(16712548685572989655)
XLA Ops:
  0.6 0.0 copy-start
  0.6 1.6 %copy-done = f32[1024,512]{1,0:T(8,128)S(1)} copy-done((f32[1024,512]{1,0:T(8,128)S(1)}, f32[1024,512]{1,0:T(8,128)}, u32[]{:S(2)}) %copy-start) | copy-done | bytes 2097176
  2.2 0.0 copy-start.2
  2.2 0.2 columns.1
  2.4 25.0 %all_to_all.30.sums_ref = f32[64,4,128]{2,1,0:T(4,128)S(1)} all-to-all(f32[64,4,128]{2,1,0:T(4,128)S(1)} %columns.1), channel_id=1, replica_groups=mesh['x'=4,'z'=8,'core'=2,'feat'=8] {'x','z','core'}, dimensions={0} | all-to-all | bytes 262144 | tf_op jit(solution)/shard_map/all_to_all | solution.py:112
  27.3 0.0 copy-start.1
  27.4 0.0 copy-done.2
  27.4 0.8 project.1
  28.2 18.8 %all_to_all.31.parts_ref = f32[8,72,128]{2,1,0:T(8,128)S(1)} all-to-all(f32[8,72,128]{2,1,0:T(8,128)S(1)} %get-tuple-element.6), channel_id=1, replica_groups=mesh['x'=4,'z'=8,'core'=2,'feat'=8] {'feat'}, dimensions={0} | all-to-all | bytes 589824 | tf_op jit(solution)/shard_map/all_to_all | solution.py:112
  47.0 13.0 %all_to_all.32.whole_ref = f32[8,72,128]{2,1,0:T(8,128)S(1)} all-to-all(f32[8,72,128]{2,1,0:T(8,128)S(1)} %normalise.1), channel_id=1, replica_groups=mesh['x'=4,'z'=8,'core'=2,'feat'=8] {'feat'}, dimensions={0} | all-to-all | bytes 589824 | tf_op jit(solution)/shard_map/all_to_all | solution.py:112
  60.0 0.0 copy-done.1
  60.0 0.7 reduce.1
  60.7 11.4 %all_to_all.33 = f32[8,8,640]{2,1,0:T(8,128)S(1)} all-to-all(f32[8,8,640]{2,1,0:T(8,128)S(1)} %bitcast.5), channel_id=1, replica_groups=mesh['x'=4,'z'=8,'core'=2,'feat'=8] {'x','core'}, dimensions={0} | all-to-all | bytes 327680 | tf_op jit(solution)/shard_map/all_to_all | solution.py:112
  72.1 10.7 %all_to_all.34 = f32[8,8,640]{2,1,0:T(8,128)S(1)} all-to-all(f32[8,8,640]{2,1,0:T(8,128)S(1)} %broadcast_in_dim.4), channel_id=1, replica_groups=mesh['x'=4,'z'=8,'core'=2,'feat'=8] {'z'}, dimensions={0} | all-to-all | bytes 327680 | tf_op jit(solution)/shard_map/all_to_all | solution.py:112
  82.9 10.4 %all_to_all.35 = f32[8,8,640]{2,1,0:T(8,128)S(1)} all-to-all(f32[8,8,640]{2,1,0:T(8,128)S(1)} %broadcast_in_dim.5), channel_id=1, replica_groups=mesh['x'=4,'z'=8,'core'=2,'feat'=8] {'x','core'}, dimensions={0} | all-to-all | bytes 327680 | tf_op jit(solution)/shard_map/all_to_all | solution.py:112
  93.2 6.4 %finish.1 = (f32[64,1024]{1,0:T(8,128)}, f32[64,512]{1,0:T(8,128)}) custom-call(f32[64,640]{1,0:T(8,128)S(1)} %bitcast.6, f32[8,72,128]{2,1,0:T(8,128)S(1)} %all_to_all.32.whole_ref, f32[1,512]{1,0:T(1,128)S(1)} %get-tuple-element.7.scale_ref), custom_call_target="tpu_custom_call" | custom-call | flops 37748736 | bytes 786432 | tf_op jit(solution)/shard_map/finish/pallas_call | solution.py:31
  (5 shorter events, 0.1 us)
Async XLA Ops:
  0.6 1.6 %copy-start = (f32[1024,512]{1,0:T(8,128)S(1)}, f32[1024,512]{1,0:T(8,128)}, u32[]{:S(2)}) copy-start(f32[1024,512]{1,0:T(8,128)} %b_ref.5) | copy-start | bytes 6291460
  2.2 25.1 %copy-start.2 = (f32[512,64]{0,1:T(8,128)S(1)}, f32[512,64]{0,1:T(8,128)}, u32[]{:S(2)}) copy-start(f32[512,64]{0,1:T(8,128)} %param.3) | copy-start | bytes 393220
  27.3 32.6 %copy-start.1 = (f32[1024,512]{1,0:T(8,128)S(1)}, f32[1024,512]{1,0:T(8,128)}, u32[]{:S(2)}) copy-start(f32[1024,512]{1,0:T(8,128)} %b_ref.5) | copy-start | bytes 6291460

commit v3 on v2

--- a/solution.py
+++ b/solution.py
@@ -1,14 +1,18 @@
+import itertools
+
 import jax
 import jax.numpy as jnp
 from jax import lax
 from jax.experimental import pallas as pl
 from jax.experimental.pallas import tpu as pltpu
-from jax.sharding import Mesh, PartitionSpec as P
+from jax.sharding import PartitionSpec as P
 
 RANK = 64
 PAD = RANK + 8
 LANES = 128
 GRID = (4, 8, 2)
+FIRST_Y = 6
+FIRST_Z = 6
 NT = (((1,), (1,)), ((), ()))
 NN = (((1,), (0,)), ((), ()))
 
@@ -77,58 +81,98 @@
     out_ref[:, cols:] = jnp.concatenate([gram, jnp.zeros((RANK, LANES - RANK), jnp.float32)], axis=1)
 
 
+def inverse_factor(gram):
+    sub = lax.broadcasted_iota(jnp.int32, (RANK, LANES), 0)
+    lane = lax.broadcasted_iota(jnp.int32, (RANK, LANES), 1)
+    diag = jnp.where(sub == lane, gram, 0.0)
+    down = lax.rsqrt(jnp.sum(diag, axis=1, keepdims=True))
+    across = lax.rsqrt(jnp.where(lane[:1] < RANK, jnp.sum(diag, axis=0, keepdims=True), 1.0))
+    full = jnp.where(lane < RANK, gram * across, (lane == RANK + sub).astype(jnp.float32)) * down
+    work = [full[8 * b : 8 * b + 8] for b in range(RANK // 8)]
+    sub = lax.broadcasted_iota(jnp.int32, (8, LANES), 0)
+    wide = (8, LANES)
+
+    def spread_row(value, s):
+        return jnp.broadcast_to(value[s : s + 1, :], wide)
+
+    out = []
+    for at in range(RANK // 8):
+        below = range(at, RANK // 8)
+        columns = {
+            i: [jnp.broadcast_to(work[i][:, 8 * at + j : 8 * at + j + 1], wide) for j in range(8)] for i in below
+        }
+        done = None
+        for s in range(0, 8, 2):
+            mine = columns[at]
+            a, b, c = spread_row(mine[s], s), spread_row(mine[s], s + 1), spread_row(mine[s + 1], s + 1)
+            top, low = spread_row(work[at], s), spread_row(work[at], s + 1)
+            det = a * c - b * b
+            inv = 1.0 / det
+            ca, cb, cc = a * inv, b * inv, c * inv
+            upper, lower = cc * top - cb * low, ca * low - cb * top
+            pairs = {}
+            for j in range(s + 2, 8):
+                tj, lj = spread_row(mine[j], s), spread_row(mine[j], s + 1)
+                pairs[j] = (cc * tj - cb * lj, ca * lj - cb * tj)
+            for i in below:
+                first, second = columns[i][s], columns[i][s + 1]
+                if i == at:
+                    first = jnp.where(sub > s + 1, first, 0.0)
+                    second = jnp.where(sub > s + 1, second, 0.0)
+                for j, (uj, wj) in pairs.items():
+                    columns[i][j] = columns[i][j] - (first * uj + second * wj)
+                work[i] = work[i] - (first * upper + second * lower)
+            ratio = 1.0 / a
+            one = top * lax.rsqrt(a)
+            two = (low - (b * ratio) * top) * lax.rsqrt(det * ratio)
+            done = one if s == 0 else jnp.where(sub == s, one, done)
+            done = jnp.where(sub == s + 1, two, done)
+        out.append(done)
+    return jnp.concatenate(out, axis=0)[:, RANK:]
+
+
 def finish_kernel(both_ref, whole_ref, scale_ref, left_ref, right_ref):
     chunks = whole_ref.shape[0]
     cols = scale_ref.shape[1]
-    sub = lax.broadcasted_iota(jnp.int32, (8, LANES), 0)
-    lane = lax.broadcasted_iota(jnp.int32, (8, LANES), 1)
-    work = [
-        jnp.where(
-            lane < RANK, both_ref[8 * b : 8 * b + 8, cols:], (lane == RANK + 8 * b + sub).astype(jnp.float32)
-        )
-        for b in range(RANK // 8)
-    ]
-    roots = [None] * (RANK // 8)
-    for k in range(RANK):
-        at, s = divmod(k, 8)
-        row = work[at][s : s + 1, :]
-        pivot = row[:, k : k + 1]
-        scaled = row * (1.0 / pivot)
-        root = jnp.broadcast_to(lax.rsqrt(pivot), (8, LANES))
-        roots[at] = root if s == 0 else jnp.where(sub == s, root, roots[at])
-        for b in range(at, RANK // 8):
-            column = work[b][:, k : k + 1]
-            if b == at:
-                column = jnp.where(sub[:, :1] > s, column, 0.0)
-            work[b] = work[b] - column * scaled
-    inverse = jnp.concatenate([work[b] * roots[b] for b in range(RANK // 8)], axis=0)[:, RANK:]
-    inverse = split(inverse)
+    inverse = split(inverse_factor(both_ref[:, cols:]))
     for i in range(chunks):
         left_ref[:, LANES * i : LANES * (i + 1)] = product(inverse, split(whole_ref[i, :RANK, :]), NN)
     right_ref[...] = product(inverse, split(both_ref[:, :cols] * scale_ref[...]), NN)
 
 
-def exchange(x, axis):
-    return lax.all_to_all(x, axis, 0, 0)
-
-
-def spread(x, axis, n):
-    return exchange(jnp.broadcast_to(x[None], (n,) + x.shape), axis)
+def groups(*order):
+    sizes = dict(zip("xzc", GRID))
+    fixed = [name for name in "xzc" if name not in order]
+
+    def lists(names):
+        return itertools.product(*[range(sizes[name]) for name in names])
+
+    def index(at):
+        return (at["x"] * sizes["z"] + (at["z"] + FIRST_Z) % sizes["z"]) * sizes["c"] + at["c"]
+
+    return [[index(dict(zip(fixed, f)) | dict(zip(order, m))) for m in lists(order)] for f in lists(fixed)]
+
+
+def exchange(x, axis, members):
+    return lax.all_to_all(x, axis, 0, 0, axis_index_groups=members)
+
+
+def spread(x, axis, members):
+    return exchange(jnp.broadcast_to(x[None], (len(members[0]),) + x.shape), axis, members)
 
 
 def body(behaviour, panel):
-    x, z, core = GRID
     feats = lax.axis_size("feat")
     rows, cols = behaviour.shape
-    cands = ("x", "z", "core")
-    near = ("x", "core")
+    every, near, far = groups("x", "z", "c"), groups("x", "c"), groups("z")
+    feat = [[(i + FIRST_Y) % feats for i in range(feats)]]
     f32 = jnp.float32
     shape = jax.ShapeDtypeStruct
 
     sums = call(
-        column_kernel, shape((x * z * core, cols // LANES, LANES), f32), (behaviour,), "columns", rows * cols, 4 * rows * cols
-    )
-    sums = exchange(sums, cands)
+        column_kernel, shape((len(every[0]), cols // LANES, LANES), f32), (behaviour,), "columns", rows * cols, 4 * rows * cols
+    )
+    sums = exchange(sums, "cand", every)
     part, col_scale = call(
         project_kernel,
         (shape((feats, PAD, rows // feats), f32), shape((1, cols), f32)),
@@ -137,18 +181,18 @@
         6 * rows * cols * PAD,
         4 * rows * cols,
     )
-    part = exchange(part, "feat")
+    part = exchange(part, "feat", feat)
     mine = call(
         normalise_kernel, shape(part.shape, f32), (part,), "normalise", part.size, 8 * part.size
     )
-    whole = exchange(mine, "feat")
+    whole = exchange(mine, "feat", feat)
     both = call(
         reduce_kernel, shape((RANK, cols + LANES), f32), (behaviour, whole), "reduce", 6 * rows * cols * RANK, 4 * rows * cols
     )
-    both = exchange(both.reshape(x * core, -1, cols + LANES), near)
+    both = exchange(both.reshape(len(near[0]), -1, cols + LANES), "cand", near)
     line = jnp.sum(both, axis=0)
-    line = jnp.sum(spread(line, "z", z), axis=0)
-    both = spread(line, near, x * core).reshape(RANK, cols + LANES)
+    line = jnp.sum(spread(line, "cand", far), axis=0)
+    both = spread(line, "cand", near).reshape(RANK, cols + LANES)
     left, right = call(
         finish_kernel,
         (shape((RANK, rows), f32), shape((RANK, cols), f32)),
@@ -162,8 +206,6 @@
 
 def solution(mesh):
     assert GRID[0] * GRID[1] * GRID[2] == mesh.shape["cand"]
-    fine = Mesh(mesh.devices.reshape(GRID + (mesh.shape["feat"],)), ("x", "z", "core", "feat"))
-    cands = ("x", "z", "core")
-    in_specs = (P(cands, "feat"), P("feat", None))
-    out_specs = (P(cands, None), P("feat", None))
-    return jax.shard_map(body, mesh=fine, in_specs=in_specs, out_specs=out_specs, check_vma=False)
+    in_specs = (P("cand", "feat"), P("feat", None))
+    out_specs = (P("cand", None), P("feat", None))
+    return jax.shard_map(body, mesh=mesh, in_specs=in_specs, out_specs=out_specs, check_vma=False)

time: 100 us -> 90.5 us (0.905)
  blocking collectives: 89.2 us -> 83.2 us
  Pallas kernels: 8.1 us -> 4.64 us
    all_to_all x6, blocking collectives: 89.2 us -> 83.2 us  [exchange(): return lax.all_to_all(x, axis, 0, 0, axis_index_groups=members)]
    pallas_call x5, Pallas kernels: 8.1 us -> 4.64 us  [call(): pl.pallas_call(kernel, out_shape=out_shape, name=name, in_specs=[pl.Block...]
where the time goes in v3:
time: 90.5 us; the launch traced here: 90.1 us
  blocking collectives  83.2 us (92%)
  Pallas kernels  4.64 us (5%)
  local copies, waits for them, and re-layouts  1.62 us (2%)
    all_to_all x6, blocking collectives, exchange(): return lax.all_to_all(x, axis, 0, 0, axis_index_groups=members)  83.2 us
    pallas_call x5, Pallas kernels, call(): pl.pallas_call(kernel, out_shape=out_shape, name=name, in_specs=[pl.Block...  4.64 us

profile of v3, /device:TPU:1, one launch (start us, length us, event | category | flops | bytes accessed | tf_op | source)
XLA Modules:
  0.0 90.1 jit_solution(14522004452693768009)
XLA Ops:
  0.6 0.0 copy-start
  0.6 1.6 %copy-done = f32[1024,512]{1,0:T(8,128)S(1)} copy-done((f32[1024,512]{1,0:T(8,128)S(1)}, f32[1024,512]{1,0:T(8,128)}, u32[]{:S(2)}) %copy-start) | copy-done | bytes 2097176
  2.2 0.0 copy-start.2
  2.2 0.2 columns.1
  2.4 23.9 %all_to_all.30.sums_ref = f32[64,4,128]{2,1,0:T(4,128)S(1)} all-to-all(f32[64,4,128]{2,1,0:T(4,128)S(1)} %columns.1), channel_id=1, replica_groups={{96,104,112,120,0,8,16,24,32,40,48,56,64,72,80,88,224,232,240,248,128,1..., dimensions={0} | all-to-all | bytes 262144 | tf_op jit(solution)/shard_map/all_to_all | solution.py:157
  26.3 0.0 copy-start.1
  26.3 0.0 copy-done.2
  26.3 0.8 project.1
  27.1 14.3 %all_to_all.31.parts_ref = f32[8,72,128]{2,1,0:T(8,128)S(1)} all-to-all(f32[8,72,128]{2,1,0:T(8,128)S(1)} %get-tuple-element.6), channel_id=1, replica_groups={{6,7,0,1,2,3,4,5},{14,15,8,9,10,11,12,13},{22,23,16,17,18,19,20,21},{30..., dimensions={0} | all-to-all | bytes 589824 | tf_op jit(solution)/shard_map/all_to_all | solution.py:157
  41.4 13.9 %all_to_all.32.whole_ref = f32[8,72,128]{2,1,0:T(8,128)S(1)} all-to-all(f32[8,72,128]{2,1,0:T(8,128)S(1)} %normalise.1), channel_id=1, replica_groups={{6,7,0,1,2,3,4,5},{14,15,8,9,10,11,12,13},{22,23,16,17,18,19,20,21},{30..., dimensions={0} | all-to-all | bytes 589824 | tf_op jit(solution)/shard_map/all_to_all | solution.py:157
  55.2 0.0 copy-done.1
  55.2 0.7 reduce.1
  55.9 11.3 %all_to_all.33 = f32[8,8,640]{2,1,0:T(8,128)S(1)} all-to-all(f32[8,8,640]{2,1,0:T(8,128)S(1)} %bitcast.5), channel_id=1, replica_groups={{96,104,224,232,352,360,480,488},{112,120,240,248,368,376,496,504},{0,8..., dimensions={0} | all-to-all | bytes 327680 | tf_op jit(solution)/shard_map/all_to_all | solution.py:157
  67.2 9.8 %all_to_all.34 = f32[8,8,640]{2,1,0:T(8,128)S(1)} all-to-all(f32[8,8,640]{2,1,0:T(8,128)S(1)} %broadcast_in_dim.4), channel_id=1, replica_groups={{96,112,0,16,32,48,64,80},{104,120,8,24,40,56,72,88},{224,240,128,144,1..., dimensions={0} | all-to-all | bytes 327680 | tf_op jit(solution)/shard_map/all_to_all | solution.py:157
  77.0 10.1 %all_to_all.35 = f32[8,8,640]{2,1,0:T(8,128)S(1)} all-to-all(f32[8,8,640]{2,1,0:T(8,128)S(1)} %broadcast_in_dim.5), channel_id=1, replica_groups={{96,104,224,232,352,360,480,488},{112,120,240,248,368,376,496,504},{0,8..., dimensions={0} | all-to-all | bytes 327680 | tf_op jit(solution)/shard_map/all_to_all | solution.py:157
  87.2 2.9 %finish.1 = (f32[64,1024]{1,0:T(8,128)}, f32[64,512]{1,0:T(8,128)}) custom-call(f32[64,640]{1,0:T(8,128)S(1)} %bitcast.6, f32[8,72,128]{2,1,0:T(8,128)S(1)} %all_to_all.32.whole_ref, f32[1,512]{1,0:T(1,128)S(1)} %get-tuple-element.7.scale_ref), custom_call_target="tpu_custom_call" | custom-call | flops 37748736 | bytes 786432 | tf_op jit(solution)/shard_map/finish/pallas_call | solution.py:35
  (5 shorter events, 0.1 us)
Async XLA Ops:
  0.6 1.6 %copy-start = (f32[1024,512]{1,0:T(8,128)S(1)}, f32[1024,512]{1,0:T(8,128)}, u32[]{:S(2)}) copy-start(f32[1024,512]{1,0:T(8,128)} %b_ref.5) | copy-start | bytes 6291460
  2.2 24.0 %copy-start.2 = (f32[512,64]{0,1:T(8,128)S(1)}, f32[512,64]{0,1:T(8,128)}, u32[]{:S(2)}) copy-start(f32[512,64]{0,1:T(8,128)} %param.3) | copy-start | bytes 393220
  26.3 29.0 %copy-start.1 = (f32[1024,512]{1,0:T(8,128)S(1)}, f32[1024,512]{1,0:T(8,128)}, u32[]{:S(2)}) copy-start(f32[1024,512]{1,0:T(8,128)} %b_ref.5) | copy-start | bytes 6291460

commit v4 on v3

--- a/solution.py
+++ b/solution.py
@@ -11,8 +11,7 @@
 PAD = RANK + 8
 LANES = 128
 GRID = (4, 8, 2)
-FIRST_Y = 6
-FIRST_Z = 6
+FIRST_X, FIRST_Y, FIRST_Z = 2, 6, 6
 NT = (((1,), (1,)), ((), ()))
 NN = (((1,), (0,)), ((), ()))
 
@@ -95,30 +94,40 @@
     def spread_row(value, s):
         return jnp.broadcast_to(value[s : s + 1, :], wide)
 
+    def lanes_of(i, start):
+        return [jnp.broadcast_to(work[i][:, start + j : start + j + 1], wide) for j in range(8)]
+
     out = []
-    for at in range(RANK // 8):
-        below = range(at, RANK // 8)
-        columns = {
-            i: [jnp.broadcast_to(work[i][:, 8 * at + j : 8 * at + j + 1], wide) for j in range(8)] for i in below
-        }
+    blocks = RANK // 8
+    mine = lanes_of(0, 0)
+    for at in range(blocks):
+        below = range(at + 1, blocks)
+        columns = {i: lanes_of(i, 8 * at) for i in below}
+        ahead = lanes_of(at + 1, 8 * at + 8) if below else []
         done = None
         for s in range(0, 8, 2):
-            mine = columns[at]
             a, b, c = spread_row(mine[s], s), spread_row(mine[s], s + 1), spread_row(mine[s + 1], s + 1)
             top, low = spread_row(work[at], s), spread_row(work[at], s + 1)
             det = a * c - b * b
             inv = 1.0 / det
             ca, cb, cc = a * inv, b * inv, c * inv
             upper, lower = cc * top - cb * low, ca * low - cb * top
+            first = jnp.where(sub > s + 1, mine[s], 0.0)
+            second = jnp.where(sub > s + 1, mine[s + 1], 0.0)
             pairs = {}
             for j in range(s + 2, 8):
-                tj, lj = spread_row(mine[j], s), spread_row(mine[j], s + 1)
-                pairs[j] = (cc * tj - cb * lj, ca * lj - cb * tj)
+                tj, lj = spread_row(mine[s], j), spread_row(mine[s + 1], j)
+                uj, wj = cc * tj - cb * lj, ca * lj - cb * tj
+                pairs[j] = uj, wj
+                mine[j] = mine[j] - (first * uj + second * wj)
+            work[at] = work[at] - (first * upper + second * lower)
+            if below:
+                first, second = columns[at + 1][s], columns[at + 1][s + 1]
+                for j in range(8):
+                    tj, lj = spread_row(first, j), spread_row(second, j)
+                    ahead[j] = ahead[j] - (first * (cc * tj - cb * lj) + second * (ca * lj - cb * tj))
             for i in below:
                 first, second = columns[i][s], columns[i][s + 1]
-                if i == at:
-                    first = jnp.where(sub > s + 1, first, 0.0)
-                    second = jnp.where(sub > s + 1, second, 0.0)
                 for j, (uj, wj) in pairs.items():
                     columns[i][j] = columns[i][j] - (first * uj + second * wj)
                 work[i] = work[i] - (first * upper + second * lower)
@@ -128,16 +137,20 @@
             done = one if s == 0 else jnp.where(sub == s, one, done)
             done = jnp.where(sub == s + 1, two, done)
         out.append(done)
+        mine = ahead
     return jnp.concatenate(out, axis=0)[:, RANK:]
 
 
 def finish_kernel(both_ref, whole_ref, scale_ref, left_ref, right_ref):
     chunks = whole_ref.shape[0]
     cols = scale_ref.shape[1]
-    inverse = split(inverse_factor(both_ref[:, cols:]))
-    for i in range(chunks):
-        left_ref[:, LANES * i : LANES * (i + 1)] = product(inverse, split(whole_ref[i, :RANK, :]), NN)
-    right_ref[...] = product(inverse, split(both_ref[:, :cols] * scale_ref[...]), NN)
+    inverse = inverse_factor(both_ref[:, cols:])
+    sides = [whole_ref[i, :RANK, :] for i in range(chunks)] + [both_ref[:, :cols] * scale_ref[...]]
+    solved = lax.dot_general(
+        inverse, jnp.concatenate(sides, axis=1), NN, precision=lax.Precision.HIGHEST, preferred_element_type=jnp.float32
+    )
+    left_ref[...] = solved[:, : chunks * LANES]
+    right_ref[...] = solved[:, chunks * LANES :]
 
 
 def groups(*order):
@@ -148,7 +161,8 @@
         return itertools.product(*[range(sizes[name]) for name in names])
 
     def index(at):
-        return (at["x"] * sizes["z"] + (at["z"] + FIRST_Z) % sizes["z"]) * sizes["c"] + at["c"]
+        x, z = (at["x"] + FIRST_X) % sizes["x"], (at["z"] + FIRST_Z) % sizes["z"]
+        return (x * sizes["z"] + z) * sizes["c"] + at["c"]
 
     return [[index(dict(zip(fixed, f)) | dict(zip(order, m))) for m in lists(order)] for f in lists(fixed)]
 

time: 90.5 us -> 88.2 us (0.975)
  blocking collectives: 83.2 us -> 81.1 us
    all_to_all x6, blocking collectives: 83.2 us -> 81.1 us  [exchange(): return lax.all_to_all(x, axis, 0, 0, axis_index_groups=members)]
where the time goes in v4:
time: 88.2 us; the launch traced here: 87.8 us
  blocking collectives  81.1 us (92%)
  Pallas kernels  4.37 us (5%)
  local copies, waits for them, and re-layouts  1.62 us (2%)
    all_to_all x6, blocking collectives, exchange(): return lax.all_to_all(x, axis, 0, 0, axis_index_groups=members)  81.1 us
    pallas_call x5, Pallas kernels, call(): pl.pallas_call(kernel, out_shape=out_shape, name=name, in_specs=[pl.Block...  4.37 us

profile of v4, /device:TPU:1, one launch (start us, length us, event | category | flops | bytes accessed | tf_op | source)
XLA Modules:
  0.0 87.8 jit_solution(17039022845178358505)
XLA Ops:
  0.6 0.0 copy-start
  0.6 1.6 %copy-done = f32[1024,512]{1,0:T(8,128)S(1)} copy-done((f32[1024,512]{1,0:T(8,128)S(1)}, f32[1024,512]{1,0:T(8,128)}, u32[]{:S(2)}) %copy-start) | copy-done | bytes 2097176
  2.2 0.0 copy-start.2
  2.2 0.2 columns.1
  2.4 21.9 %all_to_all.30.sums_ref = f32[64,4,128]{2,1,0:T(4,128)S(1)} all-to-all(f32[64,4,128]{2,1,0:T(4,128)S(1)} %columns.1), channel_id=1, replica_groups={{352,360,368,376,256,264,272,280,288,296,304,312,320,328,336,344,480,48..., dimensions={0} | all-to-all | bytes 262144 | tf_op jit(solution)/shard_map/all_to_all | solution.py:171
  24.2 0.0 copy-start.1
  24.2 0.0 copy-done.2
  24.2 0.8 project.1
  25.1 14.2 %all_to_all.31.parts_ref = f32[8,72,128]{2,1,0:T(8,128)S(1)} all-to-all(f32[8,72,128]{2,1,0:T(8,128)S(1)} %get-tuple-element.6), channel_id=1, replica_groups={{6,7,0,1,2,3,4,5},{14,15,8,9,10,11,12,13},{22,23,16,17,18,19,20,21},{30..., dimensions={0} | all-to-all | bytes 589824 | tf_op jit(solution)/shard_map/all_to_all | solution.py:171
  39.3 13.3 %all_to_all.32.whole_ref = f32[8,72,128]{2,1,0:T(8,128)S(1)} all-to-all(f32[8,72,128]{2,1,0:T(8,128)S(1)} %normalise.1), channel_id=1, replica_groups={{6,7,0,1,2,3,4,5},{14,15,8,9,10,11,12,13},{22,23,16,17,18,19,20,21},{30..., dimensions={0} | all-to-all | bytes 589824 | tf_op jit(solution)/shard_map/all_to_all | solution.py:171
  52.6 0.0 copy-done.1
  52.6 0.7 reduce.1
  53.3 12.0 %all_to_all.33 = f32[8,8,640]{2,1,0:T(8,128)S(1)} all-to-all(f32[8,8,640]{2,1,0:T(8,128)S(1)} %bitcast.5), channel_id=1, replica_groups={{352,360,480,488,96,104,224,232},{368,376,496,504,112,120,240,248},{256..., dimensions={0} | all-to-all | bytes 327680 | tf_op jit(solution)/shard_map/all_to_all | solution.py:171
  65.3 10.2 %all_to_all.34 = f32[8,8,640]{2,1,0:T(8,128)S(1)} all-to-all(f32[8,8,640]{2,1,0:T(8,128)S(1)} %broadcast_in_dim.4), channel_id=1, replica_groups={{352,368,256,272,288,304,320,336},{360,376,264,280,296,312,328,344},{48..., dimensions={0} | all-to-all | bytes 327680 | tf_op jit(solution)/shard_map/all_to_all | solution.py:171
  75.5 9.6 %all_to_all.35 = f32[8,8,640]{2,1,0:T(8,128)S(1)} all-to-all(f32[8,8,640]{2,1,0:T(8,128)S(1)} %broadcast_in_dim.5), channel_id=1, replica_groups={{352,360,480,488,96,104,224,232},{368,376,496,504,112,120,240,248},{256..., dimensions={0} | all-to-all | bytes 327680 | tf_op jit(solution)/shard_map/all_to_all | solution.py:171
  85.1 2.7 %finish.1 = (f32[64,1024]{1,0:T(8,128)}, f32[64,512]{1,0:T(8,128)}) custom-call(f32[64,640]{1,0:T(8,128)S(1)} %bitcast.6, f32[8,72,128]{2,1,0:T(8,128)S(1)} %all_to_all.32.whole_ref, f32[1,512]{1,0:T(1,128)S(1)} %get-tuple-element.7.scale_ref), custom_call_target="tpu_custom_call" | custom-call | flops 37748736 | bytes 786432 | tf_op jit(solution)/shard_map/finish/pallas_call | solution.py:34
  (5 shorter events, 0.1 us)
Async XLA Ops:
  0.6 1.6 %copy-start = (f32[1024,512]{1,0:T(8,128)S(1)}, f32[1024,512]{1,0:T(8,128)}, u32[]{:S(2)}) copy-start(f32[1024,512]{1,0:T(8,128)} %b_ref.5) | copy-start | bytes 6291460
  2.2 22.0 %copy-start.2 = (f32[512,64]{0,1:T(8,128)S(1)}, f32[512,64]{0,1:T(8,128)}, u32[]{:S(2)}) copy-start(f32[512,64]{0,1:T(8,128)} %param.3) | copy-start | bytes 393220
  24.2 28.3 %copy-start.1 = (f32[1024,512]{1,0:T(8,128)S(1)}, f32[1024,512]{1,0:T(8,128)}, u32[]{:S(2)}) copy-start(f32[1024,512]{1,0:T(8,128)} %b_ref.5) | copy-start | bytes 6291460

commit v5 on v4

--- a/solution.py
+++ b/solution.py
@@ -49,29 +49,31 @@
     out_ref[...] = jnp.broadcast_to(rows[None], out_ref.shape)
 
 
-def project_kernel(b_ref, panel_ref, sums_ref, out_ref, scale_ref):
+def project_kernel(b_ref, panel_ref, sums_ref, out_ref, rows_ref, scale_ref):
     parts = sums_ref.shape[1]
     deg = jnp.sum(sums_ref[...], axis=0)
     deg = jnp.concatenate([deg[i : i + 1] for i in range(parts)], axis=1)
     scale = lax.rsqrt(deg)
     scale_ref[...] = scale
-    ones = jnp.ones((PAD - RANK, deg.shape[1]), jnp.float32)
+    ones = jnp.ones((8, deg.shape[1]), jnp.float32)
     left = split(jnp.concatenate([panel_ref[...] * scale, ones], axis=0))
     for i in range(out_ref.shape[0]):
-        out_ref[i] = product(left, split(b_ref[LANES * i : LANES * (i + 1), :]), NT)
-
-
-def normalise_kernel(parts_ref, out_ref):
-    total = jnp.sum(parts_ref[...], axis=0)
-    scale = lax.rsqrt(total[RANK:])
-    out = jnp.concatenate([total[:RANK] * scale[:1], scale], axis=0)
+        piece = product(left, split(b_ref[LANES * i : LANES * (i + 1), :]), NT)
+        out_ref[i] = piece[:RANK]
+        rows_ref[i : i + 1, :] = piece[RANK : RANK + 1]
+
+
+def share_kernel(parts_ref, rows_ref, out_ref):
+    out = jnp.concatenate([jnp.sum(parts_ref[...], axis=0), rows_ref[...]], axis=0)
     out_ref[...] = jnp.broadcast_to(out[None], out_ref.shape)
 
 
-def reduce_kernel(b_ref, whole_ref, out_ref):
+def reduce_kernel(b_ref, whole_ref, out_ref, raw_ref):
     chunks = whole_ref.shape[0]
-    raw = jnp.concatenate([whole_ref[i, :RANK, :] for i in range(chunks)], axis=1)
-    scale = jnp.concatenate([whole_ref[i, RANK : RANK + 1, :] for i in range(chunks)], axis=1)
+    scale = lax.rsqrt(jnp.sum(whole_ref[:, RANK:, :], axis=0))
+    scale = jnp.concatenate([scale[i : i + 1] for i in range(chunks)], axis=1)
+    raw = jnp.concatenate([whole_ref[i, :RANK, :] for i in range(chunks)], axis=1) * scale
+    raw_ref[...] = raw
     cols = b_ref.shape[1]
     out_ref[:, :cols] = product(split(raw * scale), split(b_ref[...]), NN)
     gram = lax.dot_general(
@@ -141,16 +143,15 @@
     return jnp.concatenate(out, axis=0)[:, RANK:]
 
 
-def finish_kernel(both_ref, whole_ref, scale_ref, left_ref, right_ref):
-    chunks = whole_ref.shape[0]
-    cols = scale_ref.shape[1]
+def finish_kernel(both_ref, raw_ref, scale_ref, left_ref, right_ref):
+    rows, cols = raw_ref.shape[1], scale_ref.shape[1]
     inverse = inverse_factor(both_ref[:, cols:])
-    sides = [whole_ref[i, :RANK, :] for i in range(chunks)] + [both_ref[:, :cols] * scale_ref[...]]
+    sides = jnp.concatenate([raw_ref[...], both_ref[:, :cols] * scale_ref[...]], axis=1)
     solved = lax.dot_general(
-        inverse, jnp.concatenate(sides, axis=1), NN, precision=lax.Precision.HIGHEST, preferred_element_type=jnp.float32
-    )
-    left_ref[...] = solved[:, : chunks * LANES]
-    right_ref[...] = solved[:, chunks * LANES :]
+        inverse, sides, NN, precision=lax.Precision.HIGHEST, preferred_element_type=jnp.float32
+    )
+    left_ref[...] = solved[:, :rows]
+    right_ref[...] = solved[:, rows:]
 
 
 def groups(*order):
@@ -162,7 +163,7 @@
 
     def index(at):
         x, z = (at["x"] + FIRST_X) % sizes["x"], (at["z"] + FIRST_Z) % sizes["z"]
-        return (x * sizes["z"] + z) * sizes["c"] + at["c"]
+        return (x * sizes["z"] + z) * sizes["c"] + 1 - at["c"]
 
     return [[index(dict(zip(fixed, f)) | dict(zip(order, m))) for m in lists(order)] for f in lists(fixed)]
 
@@ -178,6 +179,7 @@
 def body(behaviour, panel):
     feats = lax.axis_size("feat")
     rows, cols = behaviour.shape
+    assert rows == feats * LANES and feats == 8
     every, near, far = groups("x", "z", "c"), groups("x", "c"), groups("z")
     feat = [[(i + FIRST_Y) % feats for i in range(feats)]]
     f32 = jnp.float32
@@ -187,21 +189,26 @@
         column_kernel, shape((len(every[0]), cols // LANES, LANES), f32), (behaviour,), "columns", rows * cols, 4 * rows * cols
     )
     sums = exchange(sums, "cand", every)
-    part, col_scale = call(
+    part, row_sums, col_scale = call(
         project_kernel,
-        (shape((feats, PAD, rows // feats), f32), shape((1, cols), f32)),
+        (shape((feats, RANK, LANES), f32), shape((feats, LANES), f32), shape((1, cols), f32)),
         (behaviour, panel.T, sums),
         "project",
         6 * rows * cols * PAD,
         4 * rows * cols,
     )
     part = exchange(part, "feat", feat)
-    mine = call(
-        normalise_kernel, shape(part.shape, f32), (part,), "normalise", part.size, 8 * part.size
-    )
-    whole = exchange(mine, "feat", feat)
-    both = call(
-        reduce_kernel, shape((RANK, cols + LANES), f32), (behaviour, whole), "reduce", 6 * rows * cols * RANK, 4 * rows * cols
+    share = call(
+        share_kernel, shape((feats, PAD, LANES), f32), (part, row_sums), "share", part.size, 8 * part.size
+    )
+    whole = exchange(share, "feat", feat)
+    both, raw = call(
+        reduce_kernel,
+        (shape((RANK, cols + LANES), f32), shape((RANK, rows), f32)),
+        (behaviour, whole),
+        "reduce",
+        6 * rows * cols * RANK,
+        4 * rows * cols,
     )
     both = exchange(both.reshape(len(near[0]), -1, cols + LANES), "cand", near)
     line = jnp.sum(both, axis=0)
@@ -210,7 +217,7 @@
     left, right = call(
         finish_kernel,
         (shape((RANK, rows), f32), shape((RANK, cols), f32)),
-        (both, whole, col_scale),
+        (both, raw, col_scale),
         "finish",
         6 * RANK * RANK * (rows + cols),
         8 * RANK * (rows + cols),

time: 88.2 us -> 86.5 us (0.981)
  blocking collectives: 81.1 us -> 79.5 us
    all_to_all x6, blocking collectives: 81.1 us -> 79.5 us  [exchange(): return lax.all_to_all(x, axis, 0, 0, axis_index_groups=members)]
where the time goes in v5:
time: 86.5 us; the launch traced here: 86.2 us
  blocking collectives  79.5 us (92%)
  Pallas kernels  4.33 us (5%)
  local copies, waits for them, and re-layouts  1.62 us (2%)
    all_to_all x6, blocking collectives, exchange(): return lax.all_to_all(x, axis, 0, 0, axis_index_groups=members)  79.5 us
    pallas_call x5, Pallas kernels, call(): pl.pallas_call(kernel, out_shape=out_shape, name=name, in_specs=[pl.Block...  4.33 us

profile of v5, /device:TPU:1, one launch (start us, length us, event | category | flops | bytes accessed | tf_op | source)
XLA Modules:
  0.0 86.2 jit_solution(5720182825939021602)
XLA Ops:
  0.6 0.0 copy-start
  0.6 1.6 %copy-done = f32[1024,512]{1,0:T(8,128)S(1)} copy-done((f32[1024,512]{1,0:T(8,128)S(1)}, f32[1024,512]{1,0:T(8,128)}, u32[]{:S(2)}) %copy-start) | copy-done | bytes 2097176
  2.2 0.0 copy-start.2
  2.2 0.2 columns.1
  2.4 0.0 copy-start.1
  2.4 22.0 %all_to_all.30.sums_ref = f32[64,4,128]{2,1,0:T(4,128)S(1)} all-to-all(f32[64,4,128]{2,1,0:T(4,128)S(1)} %columns.1), channel_id=1, replica_groups={{360,352,376,368,264,256,280,272,296,288,312,304,328,320,344,336,488,48..., dimensions={0} | all-to-all | bytes 262144 | tf_op jit(solution)/shard_map/all_to_all | solution.py:172
  24.4 0.0 copy-done.2
  24.4 0.8 project.1
  25.2 13.3 %all_to_all.31.parts_ref = f32[8,64,128]{2,1,0:T(8,128)S(1)} all-to-all(f32[8,64,128]{2,1,0:T(8,128)S(1)} %get-tuple-element.9), channel_id=1, replica_groups={{6,7,0,1,2,3,4,5},{14,15,8,9,10,11,12,13},{22,23,16,17,18,19,20,21},{30..., dimensions={0} | all-to-all | bytes 524288 | tf_op jit(solution)/shard_map/all_to_all | solution.py:172
  38.5 15.9 %all_to_all.32.whole_ref = f32[8,72,128]{2,1,0:T(8,128)S(1)} all-to-all(f32[8,72,128]{2,1,0:T(8,128)S(1)} %share.1), channel_id=1, replica_groups={{6,7,0,1,2,3,4,5},{14,15,8,9,10,11,12,13},{22,23,16,17,18,19,20,21},{30..., dimensions={0} | all-to-all | bytes 589824 | tf_op jit(solution)/shard_map/all_to_all | solution.py:172
  54.4 0.0 copy-done.1
  54.4 0.7 reduce.1
  55.1 9.5 %all_to_all.33 = f32[8,8,640]{2,1,0:T(8,128)S(1)} all-to-all(f32[8,8,640]{2,1,0:T(8,128)S(1)} %bitcast.6), channel_id=1, replica_groups={{360,352,488,480,104,96,232,224},{376,368,504,496,120,112,248,240},{264..., dimensions={0} | all-to-all | bytes 327680 | tf_op jit(solution)/shard_map/all_to_all | solution.py:172
  64.6 9.4 %all_to_all.34 = f32[8,8,640]{2,1,0:T(8,128)S(1)} all-to-all(f32[8,8,640]{2,1,0:T(8,128)S(1)} %broadcast_in_dim.4), channel_id=1, replica_groups={{360,376,264,280,296,312,328,344},{352,368,256,272,288,304,320,336},{48..., dimensions={0} | all-to-all | bytes 327680 | tf_op jit(solution)/shard_map/all_to_all | solution.py:172
  74.0 9.5 %all_to_all.35 = f32[8,8,640]{2,1,0:T(8,128)S(1)} all-to-all(f32[8,8,640]{2,1,0:T(8,128)S(1)} %broadcast_in_dim.5), channel_id=1, replica_groups={{360,352,488,480,104,96,232,224},{376,368,504,496,120,112,248,240},{264..., dimensions={0} | all-to-all | bytes 327680 | tf_op jit(solution)/shard_map/all_to_all | solution.py:172
  83.5 2.7 %finish.1 = (f32[64,1024]{1,0:T(8,128)}, f32[64,512]{1,0:T(8,128)}) custom-call(f32[64,640]{1,0:T(8,128)S(1)} %bitcast.5, f32[64,1024]{1,0:T(8,128)S(1)} %get-tuple-element.12.raw_ref, f32[1,512]{1,0:T(1,128)S(1)} %get-tuple-element.13.scale_ref), custom_call_target="tpu_custom_call" | custom-call | flops 37748736 | bytes 786432 | tf_op jit(solution)/shard_map/finish/pallas_call | solution.py:34
  (5 shorter events, 0.1 us)
Async XLA Ops:
  0.6 1.6 %copy-start = (f32[1024,512]{1,0:T(8,128)S(1)}, f32[1024,512]{1,0:T(8,128)}, u32[]{:S(2)}) copy-start(f32[1024,512]{1,0:T(8,128)} %b_ref.5) | copy-start | bytes 6291460
  2.2 22.2 %copy-start.2 = (f32[512,64]{0,1:T(8,128)S(1)}, f32[512,64]{0,1:T(8,128)}, u32[]{:S(2)}) copy-start(f32[512,64]{0,1:T(8,128)} %param.3) | copy-start | bytes 393220
  2.4 52.0 %copy-start.1 = (f32[1024,512]{1,0:T(8,128)S(1)}, f32[1024,512]{1,0:T(8,128)}, u32[]{:S(2)}) copy-start(f32[1024,512]{1,0:T(8,128)} %b_ref.5) | copy-start | bytes 6291460

commit v6 on v5

--- a/solution.py
+++ b/solution.py
@@ -11,7 +11,7 @@
 PAD = RANK + 8
 LANES = 128
 GRID = (4, 8, 2)
-FIRST_X, FIRST_Y, FIRST_Z = 2, 6, 6
+FIRST_X, FIRST_Y, FIRST_Z = 2, 5, 6
 NT = (((1,), (1,)), ((), ()))
 NN = (((1,), (0,)), ((), ()))
 

time: 86.5 us -> 85.9 us (level)
  no operation moved by 1% of the time
where the time goes in v6:
time: 85.9 us; the launch traced here: 85.5 us
  blocking collectives  78.9 us (92%)
  Pallas kernels  4.33 us (5%)
  local copies, waits for them, and re-layouts  1.62 us (2%)
    all_to_all x6, blocking collectives, exchange(): return lax.all_to_all(x, axis, 0, 0, axis_index_groups=members)  78.9 us
    pallas_call x5, Pallas kernels, call(): pl.pallas_call(kernel, out_shape=out_shape, name=name, in_specs=[pl.Block...  4.33 us

profile of v6, /device:TPU:1, one launch (start us, length us, event | category | flops | bytes accessed | tf_op | source)
XLA Modules:
  0.0 85.5 jit_solution(13828612712457462843)
XLA Ops:
  0.6 0.0 copy-start
  0.6 1.6 %copy-done = f32[1024,512]{1,0:T(8,128)S(1)} copy-done((f32[1024,512]{1,0:T(8,128)S(1)}, f32[1024,512]{1,0:T(8,128)}, u32[]{:S(2)}) %copy-start) | copy-done | bytes 2097176
  2.2 0.0 copy-start.2
  2.2 0.2 columns.1
  2.4 0.0 copy-start.1
  2.4 22.0 %all_to_all.30.sums_ref = f32[64,4,128]{2,1,0:T(4,128)S(1)} all-to-all(f32[64,4,128]{2,1,0:T(4,128)S(1)} %columns.1), channel_id=1, replica_groups={{360,352,376,368,264,256,280,272,296,288,312,304,328,320,344,336,488,48..., dimensions={0} | all-to-all | bytes 262144 | tf_op jit(solution)/shard_map/all_to_all | solution.py:172
  24.4 0.0 copy-done.2
  24.4 0.8 project.1
  25.2 13.0 %all_to_all.31.parts_ref = f32[8,64,128]{2,1,0:T(8,128)S(1)} all-to-all(f32[8,64,128]{2,1,0:T(8,128)S(1)} %get-tuple-element.9), channel_id=1, replica_groups={{5,6,7,0,1,2,3,4},{13,14,15,8,9,10,11,12},{21,22,23,16,17,18,19,20},{29..., dimensions={0} | all-to-all | bytes 524288 | tf_op jit(solution)/shard_map/all_to_all | solution.py:172
  38.3 14.2 %all_to_all.32.whole_ref = f32[8,72,128]{2,1,0:T(8,128)S(1)} all-to-all(f32[8,72,128]{2,1,0:T(8,128)S(1)} %share.1), channel_id=1, replica_groups={{5,6,7,0,1,2,3,4},{13,14,15,8,9,10,11,12},{21,22,23,16,17,18,19,20},{29..., dimensions={0} | all-to-all | bytes 589824 | tf_op jit(solution)/shard_map/all_to_all | solution.py:172
  52.5 0.0 copy-done.1
  52.5 0.7 reduce.1
  53.2 10.2 %all_to_all.33 = f32[8,8,640]{2,1,0:T(8,128)S(1)} all-to-all(f32[8,8,640]{2,1,0:T(8,128)S(1)} %bitcast.6), channel_id=1, replica_groups={{360,352,488,480,104,96,232,224},{376,368,504,496,120,112,248,240},{264..., dimensions={0} | all-to-all | bytes 327680 | tf_op jit(solution)/shard_map/all_to_all | solution.py:172
  63.4 9.9 %all_to_all.34 = f32[8,8,640]{2,1,0:T(8,128)S(1)} all-to-all(f32[8,8,640]{2,1,0:T(8,128)S(1)} %broadcast_in_dim.4), channel_id=1, replica_groups={{360,376,264,280,296,312,328,344},{352,368,256,272,288,304,320,336},{48..., dimensions={0} | all-to-all | bytes 327680 | tf_op jit(solution)/shard_map/all_to_all | solution.py:172
  73.4 9.5 %all_to_all.35 = f32[8,8,640]{2,1,0:T(8,128)S(1)} all-to-all(f32[8,8,640]{2,1,0:T(8,128)S(1)} %broadcast_in_dim.5), channel_id=1, replica_groups={{360,352,488,480,104,96,232,224},{376,368,504,496,120,112,248,240},{264..., dimensions={0} | all-to-all | bytes 327680 | tf_op jit(solution)/shard_map/all_to_all | solution.py:172
  82.9 2.7 %finish.1 = (f32[64,1024]{1,0:T(8,128)}, f32[64,512]{1,0:T(8,128)}) custom-call(f32[64,640]{1,0:T(8,128)S(1)} %bitcast.5, f32[64,1024]{1,0:T(8,128)S(1)} %get-tuple-element.12.raw_ref, f32[1,512]{1,0:T(1,128)S(1)} %get-tuple-element.13.scale_ref), custom_call_target="tpu_custom_call" | custom-call | flops 37748736 | bytes 786432 | tf_op jit(solution)/shard_map/finish/pallas_call | solution.py:34
  (5 shorter events, 0.1 us)
Async XLA Ops:
  0.6 1.6 %copy-start = (f32[1024,512]{1,0:T(8,128)S(1)}, f32[1024,512]{1,0:T(8,128)}, u32[]{:S(2)}) copy-start(f32[1024,512]{1,0:T(8,128)} %b_ref.5) | copy-start | bytes 6291460
  2.2 22.2 %copy-start.2 = (f32[512,64]{0,1:T(8,128)S(1)}, f32[512,64]{0,1:T(8,128)}, u32[]{:S(2)}) copy-start(f32[512,64]{0,1:T(8,128)} %param.3) | copy-start | bytes 393220
  2.4 50.1 %copy-start.1 = (f32[1024,512]{1,0:T(8,128)S(1)}, f32[1024,512]{1,0:T(8,128)}, u32[]{:S(2)}) copy-start(f32[1024,512]{1,0:T(8,128)} %b_ref.5) | copy-start | bytes 6291460

commit v7 on v6

--- a/solution.py
+++ b/solution.py
@@ -154,7 +154,7 @@
     right_ref[...] = solved[:, rows:]
 
 
-def groups(*order):
+def groups(*order, first_x=FIRST_X, first_z=FIRST_Z):
     sizes = dict(zip("xzc", GRID))
     fixed = [name for name in "xzc" if name not in order]
 
@@ -162,7 +162,7 @@
         return itertools.product(*[range(sizes[name]) for name in names])
 
     def index(at):
-        x, z = (at["x"] + FIRST_X) % sizes["x"], (at["z"] + FIRST_Z) % sizes["z"]
+        x, z = (at["x"] + first_x) % sizes["x"], (at["z"] + first_z) % sizes["z"]
         return (x * sizes["z"] + z) * sizes["c"] + 1 - at["c"]
 
     return [[index(dict(zip(fixed, f)) | dict(zip(order, m))) for m in lists(order)] for f in lists(fixed)]
@@ -180,7 +180,7 @@
     feats = lax.axis_size("feat")
     rows, cols = behaviour.shape
     assert rows == feats * LANES and feats == 8
-    every, near, far = groups("x", "z", "c"), groups("x", "c"), groups("z")
+    every, near, far = groups("x", "z", "c"), groups("x", "c"), groups("z", first_z=5)
     feat = [[(i + FIRST_Y) % feats for i in range(feats)]]
     f32 = jnp.float32
     shape = jax.ShapeDtypeStruct

time: 85.9 us -> 86 us (level)
  no operation moved by 1% of the time
where the time goes in v7:
time: 86 us; the launch traced here: 85.7 us
  blocking collectives  79 us (92%)
  Pallas kernels  4.33 us (5%)
  local copies, waits for them, and re-layouts  1.62 us (2%)
    all_to_all x6, blocking collectives, exchange(): return lax.all_to_all(x, axis, 0, 0, axis_index_groups=members)  79 us
    pallas_call x5, Pallas kernels, call(): pl.pallas_call(kernel, out_shape=out_shape, name=name, in_specs=[pl.Block...  4.33 us

profile of v7, /device:TPU:1, one launch (start us, length us, event | category | flops | bytes accessed | tf_op | source)
XLA Modules:
  0.0 85.7 jit_solution(11251054508799868348)
XLA Ops:
  0.6 0.0 copy-start
  0.6 1.6 %copy-done = f32[1024,512]{1,0:T(8,128)S(1)} copy-done((f32[1024,512]{1,0:T(8,128)S(1)}, f32[1024,512]{1,0:T(8,128)}, u32[]{:S(2)}) %copy-start) | copy-done | bytes 2097176
  2.2 0.0 copy-start.2
  2.2 0.2 columns.1
  2.4 0.0 copy-start.1
  2.4 22.0 %all_to_all.30.sums_ref = f32[64,4,128]{2,1,0:T(4,128)S(1)} all-to-all(f32[64,4,128]{2,1,0:T(4,128)S(1)} %columns.1), channel_id=1, replica_groups={{360,352,376,368,264,256,280,272,296,288,312,304,328,320,344,336,488,48..., dimensions={0} | all-to-all | bytes 262144 | tf_op jit(solution)/shard_map/all_to_all | solution.py:172
  24.4 0.0 copy-done.2
  24.4 0.8 project.1
  25.2 13.0 %all_to_all.31.parts_ref = f32[8,64,128]{2,1,0:T(8,128)S(1)} all-to-all(f32[8,64,128]{2,1,0:T(8,128)S(1)} %get-tuple-element.9), channel_id=1, replica_groups={{5,6,7,0,1,2,3,4},{13,14,15,8,9,10,11,12},{21,22,23,16,17,18,19,20},{29..., dimensions={0} | all-to-all | bytes 524288 | tf_op jit(solution)/shard_map/all_to_all | solution.py:172
  38.3 14.2 %all_to_all.32.whole_ref = f32[8,72,128]{2,1,0:T(8,128)S(1)} all-to-all(f32[8,72,128]{2,1,0:T(8,128)S(1)} %share.1), channel_id=1, replica_groups={{5,6,7,0,1,2,3,4},{13,14,15,8,9,10,11,12},{21,22,23,16,17,18,19,20},{29..., dimensions={0} | all-to-all | bytes 589824 | tf_op jit(solution)/shard_map/all_to_all | solution.py:172
  52.5 0.0 copy-done.1
  52.5 0.7 reduce.1
  53.2 10.2 %all_to_all.33 = f32[8,8,640]{2,1,0:T(8,128)S(1)} all-to-all(f32[8,8,640]{2,1,0:T(8,128)S(1)} %bitcast.6), channel_id=1, replica_groups={{360,352,488,480,104,96,232,224},{376,368,504,496,120,112,248,240},{264..., dimensions={0} | all-to-all | bytes 327680 | tf_op jit(solution)/shard_map/all_to_all | solution.py:172
  63.4 9.7 %all_to_all.34 = f32[8,8,640]{2,1,0:T(8,128)S(1)} all-to-all(f32[8,8,640]{2,1,0:T(8,128)S(1)} %broadcast_in_dim.4), channel_id=1, replica_groups={{344,360,376,264,280,296,312,328},{336,352,368,256,272,288,304,320},{47..., dimensions={0} | all-to-all | bytes 327680 | tf_op jit(solution)/shard_map/all_to_all | solution.py:172
  73.2 9.8 %all_to_all.35 = f32[8,8,640]{2,1,0:T(8,128)S(1)} all-to-all(f32[8,8,640]{2,1,0:T(8,128)S(1)} %broadcast_in_dim.5), channel_id=1, replica_groups={{360,352,488,480,104,96,232,224},{376,368,504,496,120,112,248,240},{264..., dimensions={0} | all-to-all | bytes 327680 | tf_op jit(solution)/shard_map/all_to_all | solution.py:172
  83.0 2.7 %finish.1 = (f32[64,1024]{1,0:T(8,128)}, f32[64,512]{1,0:T(8,128)}) custom-call(f32[64,640]{1,0:T(8,128)S(1)} %bitcast.5, f32[64,1024]{1,0:T(8,128)S(1)} %get-tuple-element.12.raw_ref, f32[1,512]{1,0:T(1,128)S(1)} %get-tuple-element.13.scale_ref), custom_call_target="tpu_custom_call" | custom-call | flops 37748736 | bytes 786432 | tf_op jit(solution)/shard_map/finish/pallas_call | solution.py:34
  (5 shorter events, 0.1 us)
Async XLA Ops:
  0.6 1.6 %copy-start = (f32[1024,512]{1,0:T(8,128)S(1)}, f32[1024,512]{1,0:T(8,128)}, u32[]{:S(2)}) copy-start(f32[1024,512]{1,0:T(8,128)} %b_ref.5) | copy-start | bytes 6291460
  2.2 22.2 %copy-start.2 = (f32[512,64]{0,1:T(8,128)S(1)}, f32[512,64]{0,1:T(8,128)}, u32[]{:S(2)}) copy-start(f32[512,64]{0,1:T(8,128)} %param.3) | copy-start | bytes 393220
  2.4 50.1 %copy-start.1 = (f32[1024,512]{1,0:T(8,128)S(1)}, f32[1024,512]{1,0:T(8,128)}, u32[]{:S(2)}) copy-start(f32[1024,512]{1,0:T(8,128)} %b_ref.5) | copy-start | bytes 6291460
